TPU v7x, 32 devices: a whole 2x2x4 slice. The times are simulated.
32 devices in a mesh: groups: 2 (over x), expert: 16 (over z, y, core).
Axes of the slice: x: 2, y: 2, z: 4, core: 2. Of those that a mesh axis runs over, the one named last changes fastest.
Arguments:
- tokens: bfloat16 [4096, 2048], P(('groups', 'expert')), parts along dimension 0, may hold values from -6 to 6
- stream_type: int32 [4096], P(('groups', 'expert')), parts along dimension 0, may hold values from 0 to 1
- norm_gain: float32 [2, 2048], replicated, may hold values from 0.1 to 1.9
- expert_ids: int32 [4096, 8], P(('groups', 'expert')), parts along dimension 0, may hold values from 0 to 31, all different within a row; in each aligned block of 128 rows (0 to 127, 128 to 255, ...) at most 40 rows name the same one
- gate_weights: float32 [4096, 8], P(('groups', 'expert')), parts along dimension 0, may hold values from 0.03 to 0.4
- w_gate: bfloat16 [32, 2048, 384], P('expert'), may hold values from -0.125 to 0.125
- w_up: bfloat16 [32, 2048, 384], P('expert'), may hold values from -0.125 to 0.125
- w_down: bfloat16 [32, 384, 2048], P('expert'), may hold values from -0.3125 to 0.3125
- cotangent: bfloat16 [4096, 2048], P(('groups', 'expert')), parts along dimension 0, may hold values from -6 to 6
Outputs:
- moe_out: bfloat16 [4096, 2048], P(('groups', 'expert')), parts along dimension 0
- grad_input: bfloat16 [4096, 2048], P(('groups', 'expert')), parts along dimension 0
There are 2 independent parts, one for each index of `groups`. A program takes and returns all parts, laid end to end along the dimension named above; an argument that names none is the same for every part. Nothing has to cross between parts.
Inputs may be any that keep to these rules, and one draw needn't show every extreme that they name: `expert_ids`: among the 128 tokens of one device no expert is named more than 40 times, a bound that some block reaches; the 8 experts of a token are different.
All inputs are finite; a program needn't handle non-finite values.
Results may differ from a plain program's by a relative error of at most 0.0071.
Values may be sent and summed in bfloat16 or wider, within the bound.
A program may use at most 128 MiB of HBM per device.

v0:
```python
import jax
import jax.numpy as jnp
from jax import lax
from jax.sharding import PartitionSpec as P

SLOTS = 1280


def expert_forward(row_part, w_gate, w_up, w_down):
    gate_pre = jnp.einsum("secd,edf->secf", row_part, w_gate, preferred_element_type=jnp.float32)
    up_pre = jnp.einsum("secd,edf->secf", row_part, w_up, preferred_element_type=jnp.float32)
    sig_gate = jax.nn.sigmoid(gate_pre)
    hidden = (gate_pre * sig_gate * up_pre).astype(jnp.bfloat16)
    results = jnp.einsum(
        "secf,efd->secd", hidden, w_down, preferred_element_type=jnp.float32
    ).astype(jnp.bfloat16)
    return (gate_pre, up_pre, results)


def expert_backward(gate_pre, up_pre, grad_part, w_gate, w_up, w_down):
    hidden_grad = jnp.einsum(
        "secd,efd->secf", grad_part, w_down, preferred_element_type=jnp.float32
    )
    sig_gate = jax.nn.sigmoid(gate_pre)
    pre_grad = (hidden_grad * up_pre * sig_gate * (1.0 + gate_pre * (1.0 - sig_gate))).astype(
        jnp.bfloat16
    )
    up_grad = (hidden_grad * gate_pre * sig_gate).astype(jnp.bfloat16)
    row_grad = jnp.einsum("secf,edf->secd", pre_grad, w_gate, preferred_element_type=jnp.float32)
    row_grad = row_grad + jnp.einsum(
        "secf,edf->secd", up_grad, w_up, preferred_element_type=jnp.float32
    )
    return row_grad.astype(jnp.bfloat16)


def local(
    tokens, stream_type, norm_gain, expert_ids, gate_weights, w_gate, w_up, w_down, cotangent
):
    tok_rows, model_width = tokens.shape
    top_count = expert_ids.shape[1]
    devices = lax.axis_size("expert")
    local_count = w_gate.shape[0]
    experts_all = local_count * devices
    capacity = SLOTS // experts_all
    values = tokens.astype(jnp.float32)
    inv_rms = lax.rsqrt(jnp.mean(values * values, axis=-1, keepdims=True) + 1e-06)
    unit_rows = values * inv_rms
    gain_rows = jnp.where(stream_type[:, None] == 0, norm_gain[0][None, :], norm_gain[1][None, :])
    normed = (unit_rows * gain_rows).astype(jnp.bfloat16)
    flat_ids = expert_ids.reshape(-1)
    onehot = (flat_ids[:, None] == jnp.arange(experts_all, dtype=jnp.int32)[None, :]).astype(
        jnp.int32
    )
    slot_rank = jnp.sum((jnp.cumsum(onehot, axis=0) - onehot) * onehot, axis=1)
    slot_index = flat_ids * capacity + slot_rank
    buffer_shape = (devices, local_count, capacity, model_width)

    def place(row_values):
        empty = jnp.zeros((experts_all * capacity, model_width), jnp.bfloat16)
        return empty.at[slot_index].set(row_values).reshape(buffer_shape)

    send_rows = place(jnp.repeat(normed, top_count, axis=0))
    out_grads = (gate_weights[:, :, None] * cotangent.astype(jnp.float32)[:, None, :]).astype(
        jnp.bfloat16
    )
    send_grads = place(out_grads.reshape(-1, model_width))
    arrived = lax.all_to_all(send_rows, "expert", split_axis=0, concat_axis=0, tiled=True)
    gate_pre, up_pre, results = expert_forward(arrived, w_gate, w_up, w_down)
    returned = lax.all_to_all(results, "expert", split_axis=0, concat_axis=0, tiled=True)
    grads_in = lax.all_to_all(send_grads, "expert", split_axis=0, concat_axis=0, tiled=True)
    row_grads = expert_backward(gate_pre, up_pre, grads_in, w_gate, w_up, w_down)
    grads_home = lax.all_to_all(row_grads, "expert", split_axis=0, concat_axis=0, tiled=True)
    picked = returned.reshape(-1, model_width)[slot_index].reshape(tok_rows, top_count, model_width)
    moe_out = jnp.sum(gate_weights[:, :, None] * picked.astype(jnp.float32), axis=1).astype(
        jnp.bfloat16
    )
    grad_rows = grads_home.reshape(-1, model_width)[slot_index].reshape(
        tok_rows, top_count, model_width
    )
    normed_grad = jnp.sum(grad_rows.astype(jnp.float32), axis=1)
    scaled = normed_grad * gain_rows
    grad_input = inv_rms * (
        scaled - unit_rows * jnp.mean(scaled * unit_rows, axis=-1, keepdims=True)
    )
    return (moe_out, grad_input.astype(jnp.bfloat16))


def solution(mesh):
    in_specs = (
        P(("groups", "expert"), None),
        P(("groups", "expert")),
        P(),
        P(("groups", "expert"), None),
        P(("groups", "expert"), None),
        P("expert", None, None),
        P("expert", None, None),
        P("expert", None, None),
        P(("groups", "expert"), None),
    )
    out_specs = (P(("groups", "expert"), None), P(("groups", "expert"), None))
    return jax.shard_map(local, mesh=mesh, in_specs=in_specs, out_specs=out_specs, check_vma=False)
```

profile of v0, /device:TPU:13, one launch (start us, length us, event | category | flops | bytes accessed | tf_op | source)
XLA Modules:
  0.0 527.2 jit_solution(14295730471111315002)
XLA Ops:
  0.6 0.0 copy-start
  0.6 0.8 broadcast_multiply_fusion
  1.5 0.9 copy.25
  2.4 0.1 eq.36
  2.5 0.1 eq.32
  2.6 0.7 broadcast_compare_fusion
  3.2 1.2 fusion.41
  4.5 0.8 fusion.56
  5.3 0.1 copy.24
  5.4 0.1 mul.106
  5.5 9.0 %reduce-window.6 = s32[32,8,128]{2,1,0:T(8,128)S(1)} reduce-window(s32[32,8,128]{2,1,0:T(8,128)S(1)} %fusion.52, s32[]{:T(128)} %constant.10.clone.1), window={size=1x1x128 pad=0_0x0_0x127_0}, to_apply=%region_0.0 | reduce-window | flops 4161536 | bytes 262148 | tf_op jit(solution)/shard_map/reduce-window
  14.5 0.1 slice.20
  14.6 0.1 copy.27
  14.8 0.1 copy.28
  14.9 0.1 broadcast_add_fusion
  15.0 2.1 fusion.42
  17.1 10.1 %scatter_custom_fusion = bf16[1280,2048]{1,0:T(8,128)(2,1)} fusion(s32[1024]{0:T(1024)S(1)} %bitcast.126, bf16[]{:T(256)} %constant.8.clone.1, bf16[128,2048]{1,0:T(8,128)(2,1)} %fusion.42), kind=kCustom, calls=%fused_computation.19 | custom fusion | bytes 5767170 | tf_op jit(solution)/shard_map/scatter | solution.py:60
  27.3 0.0 copy-start.10
  27.3 6.7 %all-to-all-start = ((bf16[16,2,40,2048]{3,2,1,0:T(8,128)(2,1)}), bf16[16,2,40,2048]{3,2,1,0:T(8,128)(2,1)}, u32[]{:S(2)}, u32[]{:S(2)}) async-start(bf16[16,2,40,2048]{3,2,1,0:T(8,128)(2,1)} %bitcast.116), calls=%async_computation | async-start | bytes 10485760 | tf_op jit(solution)/shard_map/all_to_all | solution.py:67
  33.9 0.0 copy-done.10
  33.9 0.1 copy.23
  34.0 0.1 mul.115
  34.1 2.1 convert_element_type.69
  36.3 19.6 %scatter_custom_fusion.1 = bf16[1280,2048]{1,0:T(8,128)(2,1)} fusion(s32[1024]{0:T(1024)S(1)} %bitcast.127, f32[128,2048]{1,0:T(8,128)} %convert_element_type.69, f32[1024]{0:T(1024)S(1)} %mul.115, bf16[]{:T(256)} %constant.8.clone.1), kind=kCustom, calls=%fused_computation.18 | custom fusion | flops 4194304 | bytes 6295554 | tf_op jit(solution)/shard_map/scatter | solution.py:60
  55.9 93.0 %all-to-all-done = bf16[16,2,40,2048]{3,2,1,0:T(8,128)(2,1)} async-done(((bf16[16,2,40,2048]{3,2,1,0:T(8,128)(2,1)}), bf16[16,2,40,2048]{3,2,1,0:T(8,128)(2,1)}, u32[]{:S(2)}, u32[]{:S(2)}) %all-to-all-start) | async-done | bytes 5242912 | tf_op jit(solution)/shard_map/all_to_all | solution.py:67
  148.9 4.8 all-to-all-start.2
  153.6 0.0 copy-start.7
  153.6 5.9 %fusion.7 = f32[2,16,40,384]{3,2,1,0:T(8,128)S(1)} fusion(bf16[16,2,40,2048]{3,2,1,0:T(8,128)(2,1)} %all-to-all-done, bf16[2,2048,384]{2,1,0:T(8,128)(2,1)} %param.14), kind=kOutput, calls=%fused_computation.16 | convolution fusion | flops 2013265920 | bytes 10354688 | tf_op jit(solution)/shard_map/secd,edf->secf/dot_general | solution.py:10
  159.5 0.0 copy-done.7
  159.6 0.0 copy-start.3
  159.6 5.6 %fusion.5 = f32[2,16,40,384]{3,2,1,0:T(8,128)S(1)} fusion(bf16[16,2,40,2048]{3,2,1,0:T(8,128)(2,1)} %all-to-all-done, bf16[2,2048,384]{2,1,0:T(8,128)(2,1)S(1)} %copy-done.7), kind=kOutput, calls=%fused_computation.14 | convolution fusion | flops 2013265920 | bytes 10354688 | tf_op jit(solution)/shard_map/secd,edf->secf/dot_general | solution.py:11
  165.2 0.0 copy-done.3
  165.2 0.0 copy-done
  165.2 0.0 copy-start.8
  165.2 3.2 convert_bitcast_fusion
  168.4 0.0 copy-done.8
  168.4 3.2 copy.31
  171.6 97.0 %all-to-all-done.2 = bf16[16,2,40,2048]{3,2,1,0:T(8,128)(2,1)} async-done(((bf16[16,2,40,2048]{3,2,1,0:T(8,128)(2,1)}), bf16[16,2,40,2048]{3,2,1,0:T(8,128)(2,1)}, u32[]{:S(2)}, u32[]{:S(2)}) %all-to-all-start.2) | async-done | bytes 5242912 | tf_op jit(solution)/shard_map/all_to_all | solution.py:70
  268.6 4.8 all-to-all-start.1
  273.3 0.0 copy-start.4
  273.4 0.0 copy-start.6
  273.4 0.0 copy-start.9
  273.4 5.0 fusion.3
  278.4 0.0 copy-start.5
  278.4 1.3 copy-done.5
  279.7 0.0 copy-done.4
  279.7 0.0 copy-done.6
  279.7 0.0 copy-done.9
  279.7 3.1 fusion.17
  282.9 8.4 %fusion.2 = bf16[16,2,40,2048]{3,2,0,1:T(8,128)(2,1)} fusion(f32[2,16,40,2048]{3,2,1,0:T(8,128)S(1)} %fusion.17, bf16[2,2048,384]{2,1,0:T(8,128)(2,1)} %param.15, f32[2,16,40,384]{3,2,1,0:T(8,128)} %copy-done.5, f32[2,16,40,384]{3,2,1,0:T(8,128)} %copy-done.3), kind=kOutput, calls=%fused_computation.10 | convolution fusion | flops 2021457920 | bytes 22806528 | tf_op jit(solution)/shard_map/secf,edf->secd/dot_general | solution.py:30
  291.3 5.7 %copy.34 = bf16[16,2,40,2048]{3,2,1,0:T(8,128)(2,1)} copy(bf16[16,2,40,2048]{3,2,0,1:T(8,128)(2,1)} %fusion.2) | data formatting | bytes 10485760 | tf_op jit(solution)/shard_map/convert_element_type | solution.py:33
  297.0 91.3 %all-to-all-done.1 = bf16[16,2,40,2048]{3,2,1,0:T(8,128)(2,1)} async-done(((bf16[16,2,40,2048]{3,2,1,0:T(8,128)(2,1)}), bf16[16,2,40,2048]{3,2,1,0:T(8,128)(2,1)}, u32[]{:S(2)}, u32[]{:S(2)}) %all-to-all-start.1) | async-done | bytes 5242912 | tf_op jit(solution)/shard_map/all_to_all | solution.py:69
  388.3 4.8 all-to-all-start.3
  393.1 12.0 %gather_fusion = bf16[1024,2048]{1,0:T(8,128)(2,1)} fusion(bf16[1280,2048]{1,0:T(8,128)(2,1)} %bitcast.17, s32[1024]{0:T(1024)S(1)} %broadcast_clamp_fusion), kind=kCustom, calls=%fused_computation | custom fusion | bytes 8392704 | tf_op jit(solution)/shard_map/gather | solution.py:73
  405.1 7.3 %fusion = bf16[128,2048]{1,0:T(8,128)(2,1)} fusion(bf16[1024,2048]{1,0:T(8,128)(2,1)} %gather_fusion, f32[128,8]{1,0:T(8,128)S(1)} %copy.23), kind=kLoop, calls=%fused_computation.7 | loop fusion | flops 6029312 | bytes 4722688 | tf_op jit(solution)/shard_map/reduce_sum | solution.py:74
  412.4 95.6 %all-to-all-done.3 = bf16[16,2,40,2048]{3,2,1,0:T(8,128)(2,1)} async-done(((bf16[16,2,40,2048]{3,2,1,0:T(8,128)(2,1)}), bf16[16,2,40,2048]{3,2,1,0:T(8,128)(2,1)}, u32[]{:S(2)}, u32[]{:S(2)}) %all-to-all-start.3) | async-done | bytes 5242912 | tf_op jit(solution)/shard_map/all_to_all | solution.py:72
  508.0 0.0 copy-start.1
  508.0 12.1 %gather_fusion.1 = bf16[1024,2048]{1,0:T(8,128)(2,1)} fusion(bf16[1280,2048]{1,0:T(8,128)(2,1)} %bitcast.26, s32[1024]{0:T(1024)S(1)} %broadcast_clamp_fusion), kind=kCustom, calls=%fused_computation.1 | custom fusion | bytes 8392704 | tf_op jit(solution)/shard_map/gather | solution.py:77
  520.1 0.0 copy-start.2
  520.1 5.1 convert_reduce_fusion
  525.3 0.0 copy-done.2
  525.3 0.4 fusion.37
  525.6 1.2 fusion.40
  526.8 0.0 copy-done.1
  (8 shorter events, 0.1 us)
Async XLA Ops:
  0.6 164.6 %copy-start = (bf16[2,384,2048]{2,1,0:T(8,128)(2,1)S(1)}, bf16[2,384,2048]{2,1,0:T(8,128)(2,1)}, u32[]{:S(2)}) copy-start(bf16[2,384,2048]{2,1,0:T(8,128)(2,1)} %param.16) | copy-start | bytes 9437188
  27.3 6.7 %copy-start.10 = (f32[128,8]{0,1:T(8,128)S(1)}, f32[128,8]{0,1:T(8,128)}, u32[]{:S(2)}) copy-start(f32[128,8]{0,1:T(8,128)} %param.13) | copy-start | bytes 12292
  27.3 121.6 %all-to-all-start = ((bf16[16,2,40,2048]{3,2,1,0:T(8,128)(2,1)}), bf16[16,2,40,2048]{3,2,1,0:T(8,128)(2,1)}, u32[]{:S(2)}, u32[]{:S(2)}) async-start(bf16[16,2,40,2048]{3,2,1,0:T(8,128)(2,1)} %bitcast.116), calls=%async_computation | async-start | bytes 10485760 | tf_op jit(solution)/shard_map/all_to_all | solution.py:67
  148.9 119.7 %all-to-all-start.2 = ((bf16[16,2,40,2048]{3,2,1,0:T(8,128)(2,1)}), bf16[16,2,40,2048]{3,2,1,0:T(8,128)(2,1)}, u32[]{:S(2)}, u32[]{:S(2)}) async-start(bf16[16,2,40,2048]{3,2,1,0:T(8,128)(2,1)} %bitcast.115), calls=%async_computation.2 | async-start | bytes 10485760 | tf_op jit(solution)/shard_map/all_to_all | solution.py:70
  153.6 5.9 %copy-start.7 = (bf16[2,2048,384]{2,1,0:T(8,128)(2,1)S(1)}, bf16[2,2048,384]{2,1,0:T(8,128)(2,1)}, u32[]{:S(2)}) copy-start(bf16[2,2048,384]{2,1,0:T(8,128)(2,1)} %param.15) | copy-start | bytes 9437188
  159.6 5.6 %copy-start.3 = (f32[2,16,40,384]{3,2,1,0:T(8,128)}, f32[2,16,40,384]{3,2,1,0:T(8,128)S(1)}, u32[]{:S(2)}) copy-start(f32[2,16,40,384]{3,2,1,0:T(8,128)S(1)} %fusion.7) | copy-start | bytes 5898244
  165.2 3.2 copy-start.8
  268.6 119.7 %all-to-all-start.1 = ((bf16[16,2,40,2048]{3,2,1,0:T(8,128)(2,1)}), bf16[16,2,40,2048]{3,2,1,0:T(8,128)(2,1)}, u32[]{:S(2)}, u32[]{:S(2)}) async-start(bf16[16,2,40,2048]{3,2,1,0:T(8,128)(2,1)} %copy.31), calls=%async_computation.1 | async-start | bytes 10485760 | tf_op jit(solution)/shard_map/all_to_all | solution.py:69
  273.3 6.4 %copy-start.4 = (f32[2,16,40,384]{3,2,1,0:T(8,128)S(1)}, f32[2,16,40,384]{3,2,1,0:T(8,128)}, u32[]{:S(2)}) copy-start(f32[2,16,40,384]{3,2,1,0:T(8,128)} %copy-done.3) | copy-start | bytes 5898244
  273.4 6.4 %copy-start.6 = (bf16[2,2048,384]{2,1,0:T(8,128)(2,1)S(1)}, bf16[2,2048,384]{2,1,0:T(8,128)(2,1)}, u32[]{:S(2)}) copy-start(bf16[2,2048,384]{2,1,0:T(8,128)(2,1)} %param.14) | copy-start | bytes 9437188
  273.4 6.4 %copy-start.9 = (f32[2,16,40,384]{3,2,1,0:T(8,128)S(1)}, f32[2,16,40,384]{3,2,1,0:T(8,128)}, u32[]{:S(2)}) copy-start(f32[2,16,40,384]{3,2,1,0:T(8,128)} %copy-done.8) | copy-start | bytes 5898244
  278.4 1.3 copy-start.5
  388.3 119.7 %all-to-all-start.3 = ((bf16[16,2,40,2048]{3,2,1,0:T(8,128)(2,1)}), bf16[16,2,40,2048]{3,2,1,0:T(8,128)(2,1)}, u32[]{:S(2)}, u32[]{:S(2)}) async-start(bf16[16,2,40,2048]{3,2,1,0:T(8,128)(2,1)} %copy.34), calls=%async_computation.3 | async-start | bytes 10485760 | tf_op jit(solution)/shard_map/all_to_all | solution.py:72
  508.0 18.8 %copy-start.1 = (bf16[2,384,2048]{2,1,0:T(8,128)(2,1)S(1)}, bf16[2,384,2048]{2,1,0:T(8,128)(2,1)}, u32[]{:S(2)}) copy-start(bf16[2,384,2048]{2,1,0:T(8,128)(2,1)} %param.16) | copy-start | bytes 9437188
  520.1 5.1 copy-start.2
where the time goes:
time: 536 us; the launch traced here: 527 us
  waiting for transfers between devices  377 us (70%)
  other arithmetic  49.8 us (9%)
  local copies, waits for them, and re-layouts  47.1 us (9%)
  matrix products  31.2 us (6%)
  starting transfers between devices  21 us (4%)
    all_to_all x1, waiting for transfers between devices, local(): lax.all_to_all(send_grads, 'expert', split_axis=0, concat_axis=0, tiled=T...  97 us
    all_to_all x1, waiting for transfers between devices, local(): lax.all_to_all(row_grads, 'expert', split_axis=0, concat_axis=0, tiled=True)  95.6 us
    all_to_all x1, waiting for transfers between devices, local(): lax.all_to_all(send_rows, 'expert', split_axis=0, concat_axis=0, tiled=True)  93 us
    all_to_all x1, waiting for transfers between devices, local(): lax.all_to_all(results, 'expert', split_axis=0, concat_axis=0, tiled=True)  91.3 us
    scatter x1, other arithmetic, place(): return empty.at[slot_index].set(row_values).reshape(buffer_shape)  19.6 us
    gather x1, local copies, waits for them, and re-layouts, local(): grads_home.reshape(-1, model_width)[slot_index]  12.1 us
    gather x1, local copies, waits for them, and re-layouts, local(): returned.reshape(-1, model_width)[slot_index]  12 us
  transfers between devices with their start and end apart: 4, of which 4 were waited for; matrix products, arithmetic and copies ran while one was open for 15% of the time, Pallas kernels for 0%

commit v1 on v0

v1 whole, which is shorter than its diff:
```python
import functools

import jax
import jax.numpy as jnp
from jax import lax
from jax.experimental import pallas as pl
from jax.experimental.pallas import tpu as pltpu
from jax.sharding import PartitionSpec as P

SLOTS = 1280
BF16 = jnp.bfloat16
F32 = jnp.float32


def dot(a, b, dims=((1,), (0,))):
    return lax.dot_general(a, b, (dims, ((), ())), preferred_element_type=F32)


def pick_table(ids, gates, first_expert, experts, cap, block):
    top, pair = ids.shape
    rows_i = lax.broadcasted_iota(jnp.int32, (pair, pair), 0)
    cols_i = lax.broadcasted_iota(jnp.int32, (pair, pair), 1)
    before = ((rows_i < cols_i) & ((rows_i < block) == (cols_i < block))).astype(BF16)
    masks = []
    weights = []
    for e in range(experts):
        hit = ids == (first_expert + e)
        masks.append(jnp.sum(hit.astype(F32), axis=0, keepdims=True))
        weights.append(jnp.sum(jnp.where(hit, gates, 0.0), axis=0, keepdims=True))
    lane = lax.broadcasted_iota(jnp.int32, (1, pair), 1)
    half = jnp.where(lane < block, 0, cap)
    slot_i = lax.broadcasted_iota(jnp.int32, (2 * cap, pair), 0)
    tables = []
    slot_weights = []
    for e in range(experts):
        rank = dot(jnp.broadcast_to(masks[e], (16, pair)).astype(BF16), before)[0:1].astype(jnp.int32)
        slot = jnp.where(masks[e] > 0.5, rank + half, -1)
        table = slot_i == slot
        tables.append(table.astype(F32))
        slot_weights.append(jnp.sum(jnp.where(table, weights[e], 0.0), axis=1, keepdims=True))
    return tables, slot_weights


def fwd_kernel(experts, cap, block, pairs, rows_ref, meta_ref, wg_ref, wu_ref, wd_ref,
               out_ref, gate_ref, up_ref, tab_ref, sw_ref, picked, weighted):
    first = lax.axis_index("expert") * experts
    top = meta_ref.shape[1] // 2
    n = 2 * cap
    for p in range(pairs):
        ids = meta_ref[p, 0:top, :]
        gates = meta_ref[p, top:, :]
        tables, slot_weights = pick_table(ids, gates, first.astype(F32), experts, cap, block)
        full = jnp.concatenate(tables, axis=0).astype(BF16)
        tab_ref[p] = full
        got = dot(full, rows_ref[p * 2 * block:(p + 1) * 2 * block, :]).astype(BF16)
        for e in range(experts):
            picked[e, p * n:(p + 1) * n, :] = got[e * n:(e + 1) * n]
            sw_ref[e, p * n:(p + 1) * n, :] = slot_weights[e]
    for e in range(experts):
        gate = dot(picked[e], wg_ref[e])
        up = dot(picked[e], wu_ref[e])
        gate_ref[e] = gate
        up_ref[e] = up
        hidden = (gate * jax.nn.sigmoid(gate) * up).astype(BF16)
        res = dot(hidden, wd_ref[e]) * sw_ref[e]
        res = res.astype(BF16)
        for p in range(pairs):
            weighted[p, e * n:(e + 1) * n, :] = res[p * n:(p + 1) * n]
    for p in range(pairs):
        out_ref[p * 2 * block:(p + 1) * 2 * block, :] = dot(
            tab_ref[p], weighted[p], ((0,), (0,))).astype(BF16)


def bwd_kernel(experts, cap, block, pairs, cot_ref, gate_ref, up_ref, tab_ref, sw_ref,
               wg_ref, wu_ref, wd_ref, out_ref, picked, weighted):
    n = 2 * cap
    tr = ((1,), (1,))
    for p in range(pairs):
        got = dot(tab_ref[p], cot_ref[p * 2 * block:(p + 1) * 2 * block, :])
        for e in range(experts):
            picked[e, p * n:(p + 1) * n, :] = (
                got[e * n:(e + 1) * n] * sw_ref[e, p * n:(p + 1) * n, :]).astype(BF16)
    for e in range(experts):
        hidden_grad = dot(picked[e], wd_ref[e], tr)
        gate = gate_ref[e]
        up = up_ref[e]
        sig = jax.nn.sigmoid(gate)
        pre_grad = (hidden_grad * up * sig * (1.0 + gate * (1.0 - sig))).astype(BF16)
        up_grad = (hidden_grad * gate * sig).astype(BF16)
        res = (dot(pre_grad, wg_ref[e], tr) + dot(up_grad, wu_ref[e], tr)).astype(BF16)
        for p in range(pairs):
            weighted[p, e * n:(e + 1) * n, :] = res[p * n:(p + 1) * n]
    for p in range(pairs):
        out_ref[p * 2 * block:(p + 1) * 2 * block, :] = dot(
            tab_ref[p], weighted[p], ((0,), (0,))).astype(BF16)


def expert_calls(meta, weights, block, cap, step_pairs):
    w_gate, w_up, w_down = weights
    experts, width, ff = w_gate.shape
    all_pairs, top2, pair = meta.shape
    grid = (all_pairs // step_pairs,)
    n = 2 * cap
    rows_spec = pl.BlockSpec((step_pairs * pair, width), lambda i: (i, 0))
    whole = lambda a: pl.BlockSpec(a.shape, lambda i: (0, 0, 0), pipeline_mode=pl.Buffered(1))
    pre_spec = pl.BlockSpec((experts, step_pairs * n, ff), lambda i: (0, i, 0))
    tab_spec = pl.BlockSpec((step_pairs, experts * n, pair), lambda i: (i, 0, 0))
    sw_spec = pl.BlockSpec((experts, step_pairs * n, 1), lambda i: (0, i, 0))
    pre_shape = jax.ShapeDtypeStruct((experts, all_pairs * n, ff), F32)
    scratch = [pltpu.VMEM((experts, step_pairs * n, width), BF16),
               pltpu.VMEM((step_pairs, experts * n, width), BF16)]
    params = pltpu.CompilerParams(vmem_limit_bytes=60 << 20)
    flops = 2 * 3 * experts * all_pairs * n * width * ff
    cost = pl.CostEstimate(flops=2 * flops, bytes_accessed=30 << 20, transcendentals=0)

    def fwd(rows):
        return pl.pallas_call(
            functools.partial(fwd_kernel, experts, cap, block, step_pairs),
            grid=grid,
            in_specs=[rows_spec, pl.BlockSpec((step_pairs, top2, pair), lambda i: (i, 0, 0)),
                      whole(w_gate), whole(w_up), whole(w_down)],
            out_specs=[rows_spec, pre_spec, pre_spec, tab_spec, sw_spec],
            out_shape=[jax.ShapeDtypeStruct(rows.shape, BF16), pre_shape, pre_shape,
                       jax.ShapeDtypeStruct((all_pairs, experts * n, pair), BF16),
                       jax.ShapeDtypeStruct((experts, all_pairs * n, 1), F32)],
            scratch_shapes=scratch, compiler_params=params, cost_estimate=cost,
        )(rows, meta, w_gate, w_up, w_down)

    def bwd(cots, gate_pre, up_pre, table, slot_weights):
        return pl.pallas_call(
            functools.partial(bwd_kernel, experts, cap, block, step_pairs),
            grid=grid,
            in_specs=[rows_spec, pre_spec, pre_spec, tab_spec, sw_spec,
                      whole(w_gate), whole(w_up), whole(w_down)],
            out_specs=rows_spec,
            out_shape=jax.ShapeDtypeStruct(cots.shape, BF16),
            scratch_shapes=scratch, compiler_params=params, cost_estimate=cost,
        )(cots, gate_pre, up_pre, table, slot_weights, w_gate, w_up, w_down)

    return fwd, bwd


def local(
    tokens, stream_type, norm_gain, expert_ids, gate_weights, w_gate, w_up, w_down, cotangent
):
    block, width = tokens.shape
    top = expert_ids.shape[1]
    devices = lax.axis_size("expert")
    experts_all = w_gate.shape[0] * devices
    cap = -(-(SLOTS // experts_all) // 8) * 8
    values = tokens.astype(F32)
    inv_rms = lax.rsqrt(jnp.mean(values * values, axis=-1, keepdims=True) + 1e-06)
    unit_rows = values * inv_rms
    gain_rows = jnp.where(stream_type[:, None] == 0, norm_gain[0][None, :], norm_gain[1][None, :])
    normed = (unit_rows * gain_rows).astype(BF16)
    meta = jnp.concatenate([expert_ids.astype(F32).T, gate_weights.T], axis=0)
    meta = lax.all_gather(meta, "expert", axis=0, tiled=False)
    meta = meta.reshape(devices // 2, 2, 2 * top, block).swapaxes(1, 2).reshape(
        devices // 2, 2 * top, 2 * block)
    rows = lax.all_gather(normed, "expert", axis=0, tiled=True)
    cots = lax.all_gather(cotangent, "expert", axis=0, tiled=True)
    fwd, bwd = expert_calls(meta, (w_gate, w_up, w_down), block, cap, 4)
    out_part, gate_pre, up_pre, table, slot_weights = fwd(rows)
    moe_out = lax.psum_scatter(out_part, "expert", scatter_dimension=0, tiled=True)
    grad_part = bwd(cots, gate_pre, up_pre, table, slot_weights)
    normed_grad = lax.psum_scatter(grad_part, "expert", scatter_dimension=0, tiled=True)
    scaled = normed_grad.astype(F32) * gain_rows
    grad_input = inv_rms * (
        scaled - unit_rows * jnp.mean(scaled * unit_rows, axis=-1, keepdims=True)
    )
    return (moe_out, grad_input.astype(BF16))


def solution(mesh):
    in_specs = (
        P(("groups", "expert"), None),
        P(("groups", "expert")),
        P(),
        P(("groups", "expert"), None),
        P(("groups", "expert"), None),
        P("expert", None, None),
        P("expert", None, None),
        P("expert", None, None),
        P(("groups", "expert"), None),
    )
    out_specs = (P(("groups", "expert"), None), P(("groups", "expert"), None))
    return jax.shard_map(local, mesh=mesh, in_specs=in_specs, out_specs=out_specs, check_vma=False)
```

time: 536 us -> 402 us (0.75); the launches traced: 527 us -> 400 us
  waiting for transfers between devices: 377 us -> 317 us
  local copies, waits for them, and re-layouts: 47.1 us -> 1.64 us
  Pallas kernels: 0 us -> 41.8 us
  other arithmetic: 49.8 us -> 9.12 us
  matrix products: 31.2 us -> 0 us
  starting transfers between devices: 21 us -> 0.16 us
  blocking collectives: 0 us -> 16.3 us
  between operations: 1.24 us -> 13.8 us
    all_to_all x4 -> x0, waiting for transfers between devices: 377 us -> none  [the longest x1 97 us: local(): lax.all_to_all(send_grads, 'expert', split_axis=0, concat_axis=0, tiled=T...]
    reduce_scatter x0 -> x2, waiting for transfers between devices: none -> 206 us  [the longest x1 104 us: local(): lax.psum_scatter(out_part, 'expert', scatter_dimension=0, tiled=True)]
    all_gather x0 -> x2, waiting for transfers between devices: none -> 110 us  [the longest x1 55.9 us: local(): rows = lax.all_gather(normed, 'expert', axis=0, tiled=True)]
    pallas_call x0 -> x2, Pallas kernels: none -> 41.8 us  [the longest x1 21.4 us: fwd(): pl.pallas_call(functools.partial(fwd_kernel, experts, cap, block, step_pa...]
    dot_general x6 -> x0, matrix products: 31.2 us -> none  [the longest x1 8.38 us: expert_backward(): jnp.einsum('secf,edf->secd', up_grad, w_up, preferred_element_type=jnp.fl...]
    gather x2 -> x0, local copies, waits for them, and re-layouts: 24.1 us -> none  [the longest x1 12.1 us: local(): grads_home.reshape(-1, model_width)[slot_index]]
    all_to_all x4 -> x0, starting transfers between devices: 21 us -> none  [the longest x1 6.65 us: local(): lax.all_to_all(send_rows, 'expert', split_axis=0, concat_axis=0, tiled=True)]
    scatter x1 -> x0, other arithmetic: 19.6 us -> none  [place(): return empty.at[slot_index].set(row_values).reshape(buffer_shape)]
  transfers between devices with their start and end apart: 4 -> 4, of which waited for: 4 -> 4; matrix products, arithmetic and copies ran while one was open for 15% -> 1% of each run, Pallas kernels for 0% -> 5%
where the time goes in v1:
time: 402 us; the launch traced here: 400 us
  waiting for transfers between devices  317 us (79%)
  Pallas kernels  41.8 us (10%)
  blocking collectives  16.3 us (4%)
  between operations  13.8 us (3%)
  other arithmetic  9.12 us (2%)
    reduce_scatter x1, waiting for transfers between devices, local(): lax.psum_scatter(out_part, 'expert', scatter_dimension=0, tiled=True)  104 us
    reduce_scatter x1, waiting for transfers between devices, local(): lax.psum_scatter(grad_part, 'expert', scatter_dimension=0, tiled=True)  102 us
    all_gather x1, waiting for transfers between devices, local(): rows = lax.all_gather(normed, 'expert', axis=0, tiled=True)  55.9 us
    all_gather x1, waiting for transfers between devices, local(): cots = lax.all_gather(cotangent, 'expert', axis=0, tiled=True)  53.7 us
    pallas_call x1, Pallas kernels, fwd(): pl.pallas_call(functools.partial(fwd_kernel, experts, cap, block, step_pa...  21.4 us
    pallas_call x1, Pallas kernels, bwd(): pl.pallas_call(functools.partial(bwd_kernel, experts, cap, block, step_pa...  20.3 us
    all_gather x1, blocking collectives, local(): meta = lax.all_gather(meta, 'expert', axis=0, tiled=False)  16.3 us
  transfers between devices with their start and end apart: 4, of which 4 were waited for; matrix products, arithmetic and copies ran while one was open for 1% of the time, Pallas kernels for 5%

profile of v1, /device:TPU:13, one launch (start us, length us, event | category | flops | bytes accessed | tf_op | source)
XLA Modules:
  0.0 399.6 jit_solution(5831089460145940033)
XLA Ops:
  7.2 0.0 all-gather.4.cloned.1.call-start
  7.2 0.8 fusion.8
  8.0 1.2 fusion.6
  9.3 0.7 broadcast_compare_fusion
  9.9 2.1 fusion.7
  12.0 0.0 all-gather.4.cloned.1.call-update
  12.0 0.0 all-gather.6.cloned.1.call-start
  12.1 0.7 all-gather.6.cloned.1.call-update
  12.8 0.0 reduce-scatter.5.cloned.1.call-start
  12.8 0.7 convert_bitcast_fusion
  13.5 0.7 pad_maximum_fusion
  14.2 16.3 %all-gather = f32[256,128]{1,0:T(8,128)S(1)} all-gather(f32[16,128]{1,0:T(8,128)S(1)} %pad_maximum_fusion), channel_id=2, replica_groups=mesh['groups'=2,'expert'=16] {'expert'}, dimensions={0}, use_global_device_ids=true | all-gather | bytes 139264 | tf_op jit(solution)/shard_map/all_gather | solution.py:157
  30.6 0.1 copy.13
  30.6 0.8 reshape.25.meta_ref
  31.4 55.9 %all-gather.4.cloned.1.call-done.rows_ref = bf16[2048,2048]{1,0:T(8,128)(2,1)} async-done(((bf16[128,2048]{1,0:T(8,128)(2,1)}), bf16[2048,2048]{1,0:T(8,128)(2,1)}) %all-gather.4.cloned.1.call-update) | async-done | bytes 8388624 | tf_op jit(solution)/shard_map/all_gather | solution.py:160
  87.3 21.4 %shard_map.104 = (bf16[2048,2048]{1,0:T(8,128)(2,1)}, f32[2,640,384]{2,1,0:T(8,128)}, f32[2,640,384]{2,1,0:T(8,128)}, bf16[8,160,256]{2,1,0:T(8,128)(2,1)}, f32[2,640,1]{2,1,0:T(8,128)}) custom-call(bf16[2048,2048]{1,0:T(8,128)(2,1)} %all-gather.4.cloned.1.call-done.rows_ref, f32[8,16,256]{2,1,0:T(8,128)} %reshape.25.meta_ref, bf16[2,2048,384]{2,1,0:T(8,128)(2,1)} %wg_ref.3, ...), custom_call_target="tpu_custom_call" | custom-call | flops 12079595520 | bytes 31457280 | tf_op jit(solution)/shard_map/pallas_call | solution.py:117
  108.7 53.7 %all-gather.6.cloned.1.call-done.cot_ref = bf16[2048,2048]{1,0:T(8,128)(2,1)} async-done(((bf16[128,2048]{1,0:T(8,128)(2,1)}), bf16[2048,2048]{1,0:T(8,128)(2,1)}) %all-gather.6.cloned.1.call-update) | async-done | bytes 8388624 | tf_op jit(solution)/shard_map/all_gather | solution.py:161
  162.4 20.3 %shard_map.105 = bf16[2048,2048]{1,0:T(8,128)(2,1)} custom-call(bf16[2048,2048]{1,0:T(8,128)(2,1)} %all-gather.6.cloned.1.call-done.cot_ref, f32[2,640,384]{2,1,0:T(8,128)} %get-tuple-element.8.gate_ref, f32[2,640,384]{2,1,0:T(8,128)} %get-tuple-element.9.up_ref, bf16[8,160,256]{2,1,0:T(8,128)(2,1)} %get-tuple-element.10.tab_ref, ...), custom_call_target="tpu_custom_call" | custom-call | flops 12079595520 | bytes 31457280 | tf_op jit(solution)/shard_map/pallas_call | solution.py:130
  182.7 0.0 reduce-scatter.5.cloned.1.call-update
  182.7 0.0 reduce-scatter.3.cloned.1.call-start
  182.8 0.0 copy-start
  182.8 0.5 reduce-scatter.3.cloned.1.call-update
  183.3 102.2 %reduce-scatter.5.cloned.1.call-done = bf16[128,2048]{1,0:T(8,128)(2,1)} async-done(((bf16[2048,2048]{1,0:T(8,128)(2,1)}), bf16[128,2048]{1,0:T(8,128)(2,1)}) %reduce-scatter.5.cloned.1.call-update) | async-done | bytes 524304 | tf_op jit(solution)/shard_map/reduce_scatter | solution.py:166
  285.5 0.0 copy-done
  285.5 1.5 fusion.2
  287.0 2.3 fusion.5
  289.2 103.9 %reduce-scatter.3.cloned.1.call-done = bf16[128,2048]{1,0:T(8,128)(2,1)} async-done(((bf16[2048,2048]{1,0:T(8,128)(2,1)}), bf16[128,2048]{1,0:T(8,128)(2,1)}) %reduce-scatter.3.cloned.1.call-update) | async-done | bytes 524304 | tf_op jit(solution)/shard_map/reduce_scatter | solution.py:164
  (2 shorter events, 0.0 us)
Async XLA Ops:
  7.2 80.1 %all-gather.4.cloned.1.call-start = ((), (), s32[]{:S(2)}) async-start(), calls=%async_computation.2 | async-start | bytes 8912896 | tf_op jit(solution)/shard_map/all_gather | solution.py:160
  12.0 150.3 %all-gather.6.cloned.1.call-start = ((), (), s32[]{:S(2)}) async-start(), calls=%async_computation.4 | async-start | bytes 8912896 | tf_op jit(solution)/shard_map/all_gather | solution.py:161
  12.8 272.7 %reduce-scatter.5.cloned.1.call-start = ((), (), s32[]{:S(2)}) async-start(), calls=%async_computation.5 | async-start | bytes 8912896 | tf_op jit(solution)/shard_map/reduce_scatter | solution.py:166
  182.7 210.4 %reduce-scatter.3.cloned.1.call-start = ((), (), s32[]{:S(2)}) async-start(), calls=%async_computation.3 | async-start | bytes 8912896 | tf_op jit(solution)/shard_map/reduce_scatter | solution.py:164
  182.8 102.7 %copy-start = (bf16[128,2048]{1,0:T(8,128)(2,1)S(1)}, bf16[128,2048]{1,0:T(8,128)(2,1)}, u32[]{:S(2)}) copy-start(bf16[128,2048]{1,0:T(8,128)(2,1)} %param.9) | copy-start | bytes 1572868
Sparse Core Ops, SparseCore 0:
  12.2 75.0 all-gather.3
  89.4 72.8 all-gather.5
  182.8 102.6 reduce-scatter.4
  290.0 103.0 reduce-scatter.2

commit v2 on v1

--- a/solution.py
+++ b/solution.py
@@ -41,18 +41,19 @@
     return tables, slot_weights
 
 
-def fwd_kernel(experts, cap, block, pairs, rows_ref, meta_ref, wg_ref, wu_ref, wd_ref,
+def fwd_kernel(experts, cap, block, pairs, top, rows_ref, wg_ref, wu_ref, wd_ref,
                out_ref, gate_ref, up_ref, tab_ref, sw_ref, picked, weighted):
     first = lax.axis_index("expert") * experts
-    top = meta_ref.shape[1] // 2
+    width = wg_ref.shape[1]
     n = 2 * cap
     for p in range(pairs):
-        ids = meta_ref[p, 0:top, :]
-        gates = meta_ref[p, top:, :]
+        meta = rows_ref[p * 2 * block:(p + 1) * 2 * block, width:].astype(F32).T
+        ids = meta[0:top]
+        gates = (meta[top:2 * top] + meta[2 * top:3 * top]) + meta[3 * top:4 * top]
         tables, slot_weights = pick_table(ids, gates, first.astype(F32), experts, cap, block)
         full = jnp.concatenate(tables, axis=0).astype(BF16)
         tab_ref[p] = full
-        got = dot(full, rows_ref[p * 2 * block:(p + 1) * 2 * block, :]).astype(BF16)
+        got = dot(full, rows_ref[p * 2 * block:(p + 1) * 2 * block, 0:width]).astype(BF16)
         for e in range(experts):
             picked[e, p * n:(p + 1) * n, :] = got[e * n:(e + 1) * n]
             sw_ref[e, p * n:(p + 1) * n, :] = slot_weights[e]
@@ -95,10 +96,240 @@
             tab_ref[p], weighted[p], ((0,), (0,))).astype(BF16)
 
 
-def expert_calls(meta, weights, block, cap, step_pairs):
+def ring_place(chips):
+    me = lax.axis_index("expert")
+    chip = me // 2
+    core = me % 2
+    row, col = chip // 2, chip % 2
+    place = row + col * (chips - 1 - 2 * row)
+
+    def index(at, which):
+        at = (at + 2 * chips) % chips
+        back = at // (chips // 2)
+        return ((1 - back) * (2 * at) + back * (2 * (chips - 1 - at) + 1)) * 2 + which
+
+    return place, core, index
+
+
+def enter(peers):
+    barrier = pltpu.get_barrier_semaphore()
+    for peer in peers:
+        pl.semaphore_signal(barrier, inc=1, device_id={"expert": peer},
+                            device_id_type=pl.DeviceIdType.MESH)
+    pl.semaphore_wait(barrier, len(peers))
+
+
+def pieces(chips):
+    far = chips // 2
+    order = []
+    for way in range(2):
+        row = []
+        for d in range(1, far + 1):
+            row.append((d, way))
+            if d < far:
+                row.append((d, 1 - way))
+        order.append(row)
+    return order
+
+
+def send_to(src, dst, send_sem, recv_sem, peer):
+    return pltpu.make_async_remote_copy(
+        src_ref=src, dst_ref=dst, send_sem=send_sem, recv_sem=recv_sem,
+        device_id={"expert": peer}, device_id_type=pl.DeviceIdType.MESH)
+
+
+def gather_kernel(chips, a_ref, b_ref, oa_ref, ob_ref, ring_s, ring_r, pair_s, pair_r, own_s):
+    place, core, index = ring_place(chips)
+    steps = (1, -1)
+    peers = [index(place + 1, core), index(place - 1, core)]
+    partner = index(place, 1 - core)
+    enter(peers + [partner])
+    block = a_ref.shape[0]
+    half = block // 2
+    ins = (a_ref, b_ref)
+    outs = (oa_ref, ob_ref)
+    order = pieces(chips)
+    count = len(order[0])
+
+    def rows(which, at, h):
+        start = pl.multiple_of(index(at, which) * block + h * half, half)
+        return pl.ds(start, half)
+
+    waits = []
+    own = []
+    for j in range(2):
+        for x in range(2):
+            for way in range(2):
+                d, h = order[way][j]
+                here = rows(core, place, h)
+                copy = send_to(ins[x].at[pl.ds(h * half, half), :], outs[x].at[here, :],
+                               ring_s.at[x, way, j], ring_r.at[x, way, j], peers[way])
+                copy.start()
+                waits.append(copy)
+    for x in range(2):
+        here = pl.ds(pl.multiple_of(index(place, core) * block, block), block)
+        copy = pltpu.make_async_copy(ins[x], outs[x].at[here, :], own_s.at[x])
+        copy.start()
+        own.append(copy)
+        copy = send_to(ins[x], outs[x].at[here, :], pair_s.at[x, 2, 0], pair_r.at[x, 2, 0], partner)
+        copy.start()
+        waits.append(copy)
+    for j in range(count):
+        for x in range(2):
+            for way in range(2):
+                d, h = order[way][j]
+                got = outs[x].at[rows(core, place - steps[way] * d, h), :]
+                send_to(got, got, ring_s.at[x, way, j], ring_r.at[x, way, j], peers[way]).wait_recv()
+                if (d + 1, h) in order[way]:
+                    k = order[way].index((d + 1, h))
+                    copy = send_to(got, got, ring_s.at[x, way, k], ring_r.at[x, way, k], peers[way])
+                    copy.start()
+                    waits.append(copy)
+                copy = send_to(got, got, pair_s.at[x, way, j], pair_r.at[x, way, j], partner)
+                copy.start()
+                waits.append(copy)
+    for copy in waits:
+        copy.wait_send()
+    for copy in own:
+        copy.wait()
+    for x in range(2):
+        here = outs[x].at[pl.ds(pl.multiple_of(index(place, 1 - core) * block, block), block), :]
+        send_to(here, here, pair_s.at[x, 2, 0], pair_r.at[x, 2, 0], partner).wait_recv()
+        for j in range(count):
+            for way in range(2):
+                d, h = order[way][j]
+                here = outs[x].at[rows(1 - core, place - steps[way] * d, h), :]
+                send_to(here, here, pair_s.at[x, way, j], pair_r.at[x, way, j], partner).wait_recv()
+
+
+def ring_gather(a, b, devices):
+    chips = devices // 2
+    count = chips - 1
+    sems = pltpu.SemaphoreType.DMA
+    return pl.pallas_call(
+        functools.partial(gather_kernel, chips),
+        out_shape=[jax.ShapeDtypeStruct((devices * x.shape[0], x.shape[1]), x.dtype) for x in (a, b)],
+        in_specs=[pl.BlockSpec(memory_space=pltpu.VMEM)] * 2,
+        out_specs=[pl.BlockSpec(memory_space=pl.ANY)] * 2,
+        scratch_shapes=[sems((2, 2, count)), sems((2, 2, count)), sems((2, 3, count)),
+                        sems((2, 3, count)), sems((2,))],
+        compiler_params=pltpu.CompilerParams(collective_id=0, has_side_effects=True),
+    )(a, b)
+
+
+def scatter_kernel(chips, a_ref, b_ref, oa_ref, ob_ref, pair_buf, send_buf, recv_buf,
+                   ring_s, ring_r, pair_s, pair_r):
+    place, core, index = ring_place(chips)
+    steps = (1, -1)
+    peers = [index(place + 1, core), index(place - 1, core)]
+    partner = index(place, 1 - core)
+    enter(peers + [partner])
+    block = oa_ref.shape[0]
+    half = block // 2
+    ins = (a_ref, b_ref)
+    outs = (oa_ref, ob_ref)
+    far = chips // 2
+    order = [row[::-1] for row in pieces(chips)]
+    count = len(order[0])
+    offsets = [far]
+    for d in range(far - 1, 0, -1):
+        offsets += [d, -d]
+    offsets.append(0)
+    slot_of = {o: i for i, o in enumerate(offsets)}
+    slot_of[-far] = 0
+    pair_copies = {}
+    for i, o in enumerate(offsets):
+        for x in range(2):
+            theirs = pl.ds(pl.multiple_of(index(place + o, 1 - core) * block, block), block)
+            copy = send_to(ins[x].at[theirs, :], pair_buf.at[x, i], pair_s.at[x, i],
+                           pair_r.at[x, i], partner)
+            copy.start()
+            pair_copies[x, i] = copy
+    arrived = set()
+
+    def need(x, i):
+        if (x, i) not in arrived:
+            arrived.add((x, i))
+            pair_copies[x, i].wait_recv()
+
+    tile = 16
+
+    def add_up(x, o, h, more, write):
+        i = slot_of[o]
+        need(x, i)
+        base = index(place + o, core) * block + h * half
+
+        def body(t, carry):
+            r = pl.multiple_of(t * tile, tile)
+            total = ins[x][pl.ds(pl.multiple_of(base + r, tile), tile), :].astype(F32)
+            total = total + pair_buf[x, i, pl.ds(pl.multiple_of(h * half + r, tile), tile), :].astype(F32)
+            for ref in more:
+                total = total + recv_buf[ref + (pl.ds(r, tile), slice(None))].astype(F32)
+            write(r, total)
+            return carry
+
+        lax.fori_loop(0, half // tile, body, 0)
+
+    sends = {}
+    for j in range(count):
+        for x in range(2):
+            for way in range(2):
+                d, h = order[way][j]
+                more = []
+                if (d + 1, h) in order[way]:
+                    k = order[way].index((d + 1, h))
+                    sends[x, way, k].wait_recv()
+                    more.append((x, way, k))
+
+                def write(r, total, x=x, way=way, j=j):
+                    send_buf[x, way, j, pl.ds(r, tile), :] = total.astype(BF16)
+
+                add_up(x, steps[way] * d, h, more, write)
+                copy = send_to(send_buf.at[x, way, j], recv_buf.at[x, way, j],
+                               ring_s.at[x, way, j], ring_r.at[x, way, j], peers[way])
+                copy.start()
+                sends[x, way, j] = copy
+    for x in range(2):
+        for h in range(2):
+            more = []
+            for way in range(2):
+                k = order[way].index((1, h))
+                sends[x, way, k].wait_recv()
+                more.append((x, way, k))
+
+            def write(r, total, x=x, h=h):
+                outs[x][pl.ds(pl.multiple_of(h * half + r, tile), tile), :] = total.astype(outs[x].dtype)
+
+            add_up(x, 0, h, more, write)
+    for copy in sends.values():
+        copy.wait_send()
+    for copy in pair_copies.values():
+        copy.wait_send()
+
+
+def ring_scatter(a, b, devices):
+    chips = devices // 2
+    count = chips - 1
+    block, width = a.shape[0] // devices, a.shape[1]
+    sems = pltpu.SemaphoreType.DMA
+    return pl.pallas_call(
+        functools.partial(scatter_kernel, chips),
+        out_shape=[jax.ShapeDtypeStruct((block, width), BF16), jax.ShapeDtypeStruct((block, width), F32)],
+        in_specs=[pl.BlockSpec(memory_space=pltpu.VMEM)] * 2,
+        out_specs=[pl.BlockSpec(memory_space=pltpu.VMEM)] * 2,
+        scratch_shapes=[pltpu.VMEM((2, chips, block, width), BF16),
+                        pltpu.VMEM((2, 2, count, block // 2, width), BF16),
+                        pltpu.VMEM((2, 2, count, block // 2, width), BF16),
+                        sems((2, 2, count)), sems((2, 2, count)), sems((2, chips)), sems((2, chips))],
+        compiler_params=pltpu.CompilerParams(collective_id=1, has_side_effects=True,
+                                             vmem_limit_bytes=62 << 20),
+    )(a, b)
+
+
+def expert_calls(devices, top, weights, block, cap, step_pairs):
     w_gate, w_up, w_down = weights
     experts, width, ff = w_gate.shape
-    all_pairs, top2, pair = meta.shape
+    all_pairs, pair = devices // 2, 2 * block
     grid = (all_pairs // step_pairs,)
     n = 2 * cap
     rows_spec = pl.BlockSpec((step_pairs * pair, width), lambda i: (i, 0))
@@ -115,16 +346,16 @@
 
     def fwd(rows):
         return pl.pallas_call(
-            functools.partial(fwd_kernel, experts, cap, block, step_pairs),
+            functools.partial(fwd_kernel, experts, cap, block, step_pairs, top),
             grid=grid,
-            in_specs=[rows_spec, pl.BlockSpec((step_pairs, top2, pair), lambda i: (i, 0, 0)),
+            in_specs=[pl.BlockSpec((step_pairs * pair, rows.shape[1]), lambda i: (i, 0)),
                       whole(w_gate), whole(w_up), whole(w_down)],
             out_specs=[rows_spec, pre_spec, pre_spec, tab_spec, sw_spec],
-            out_shape=[jax.ShapeDtypeStruct(rows.shape, BF16), pre_shape, pre_shape,
+            out_shape=[jax.ShapeDtypeStruct((rows.shape[0], width), BF16), pre_shape, pre_shape,
                        jax.ShapeDtypeStruct((all_pairs, experts * n, pair), BF16),
                        jax.ShapeDtypeStruct((experts, all_pairs * n, 1), F32)],
             scratch_shapes=scratch, compiler_params=params, cost_estimate=cost,
-        )(rows, meta, w_gate, w_up, w_down)
+        )(rows, w_gate, w_up, w_down)
 
     def bwd(cots, gate_pre, up_pre, table, slot_weights):
         return pl.pallas_call(
@@ -153,17 +384,27 @@
     unit_rows = values * inv_rms
     gain_rows = jnp.where(stream_type[:, None] == 0, norm_gain[0][None, :], norm_gain[1][None, :])
     normed = (unit_rows * gain_rows).astype(BF16)
-    meta = jnp.concatenate([expert_ids.astype(F32).T, gate_weights.T], axis=0)
-    meta = lax.all_gather(meta, "expert", axis=0, tiled=False)
-    meta = meta.reshape(devices // 2, 2, 2 * top, block).swapaxes(1, 2).reshape(
-        devices // 2, 2 * top, 2 * block)
-    rows = lax.all_gather(normed, "expert", axis=0, tiled=True)
-    cots = lax.all_gather(cotangent, "expert", axis=0, tiled=True)
-    fwd, bwd = expert_calls(meta, (w_gate, w_up, w_down), block, cap, 4)
+    high = lax.reduce_precision(gate_weights, 8, 7)
+    middle = lax.reduce_precision(gate_weights - high, 8, 7)
+    low = gate_weights - high - middle
+    pad = jnp.zeros((block, 128 - 4 * top), BF16)
+    normed = jnp.concatenate(
+        [normed, expert_ids.astype(BF16), high.astype(BF16), middle.astype(BF16), low.astype(BF16), pad],
+        axis=1)
+    by_ring = devices % 4 == 0 and devices * block * width * 2 * 2 <= 20 << 20
+    if by_ring:
+        rows, cots = ring_gather(normed, cotangent, devices)
+    else:
+        rows = lax.all_gather(normed, "expert", axis=0, tiled=True)
+        cots = lax.all_gather(cotangent, "expert", axis=0, tiled=True)
+    fwd, bwd = expert_calls(devices, top, (w_gate, w_up, w_down), block, cap, 4)
     out_part, gate_pre, up_pre, table, slot_weights = fwd(rows)
-    moe_out = lax.psum_scatter(out_part, "expert", scatter_dimension=0, tiled=True)
     grad_part = bwd(cots, gate_pre, up_pre, table, slot_weights)
-    normed_grad = lax.psum_scatter(grad_part, "expert", scatter_dimension=0, tiled=True)
+    if by_ring:
+        moe_out, normed_grad = ring_scatter(out_part, grad_part, devices)
+    else:
+        moe_out = lax.psum_scatter(out_part, "expert", scatter_dimension=0, tiled=True)
+        normed_grad = lax.psum_scatter(grad_part, "expert", scatter_dimension=0, tiled=True)
     scaled = normed_grad.astype(F32) * gain_rows
     grad_input = inv_rms * (
         scaled - unit_rows * jnp.mean(scaled * unit_rows, axis=-1, keepdims=True)

time: 402 us -> 239 us (0.59)
  waiting for transfers between devices: 317 us -> 0 us
  Pallas kernels: 41.8 us -> 223 us
  blocking collectives: 16.3 us -> 0 us
  between operations: 13.8 us -> 0.69 us
    reduce_scatter x2 -> x0, waiting for transfers between devices: 206 us -> none  [the longest x1 104 us: local(): lax.psum_scatter(out_part, 'expert', scatter_dimension=0, tiled=True)]
    pallas_call x0 -> x2, Pallas kernels: none -> 181 us  [the longest x1 91.2 us: ring_scatter(): pl.pallas_call(functools.partial(scatter_kernel, chips), out_shape=[jax.S...]
    all_gather x2 -> x0, waiting for transfers between devices: 110 us -> none  [the longest x1 55.9 us: local(): rows = lax.all_gather(normed, 'expert', axis=0, tiled=True)]
    all_gather x1 -> x0, blocking collectives: 16.3 us -> none  [local(): meta = lax.all_gather(meta, 'expert', axis=0, tiled=False)]
  transfers between devices with their start and end apart: 4 -> 0, of which waited for: 4 -> 0; matrix products, arithmetic and copies ran while one was open for 1% -> 0% of each run, Pallas kernels for 5% -> 0%
where the time goes in v2:
time: 239 us; the launch traced here: 236 us
  Pallas kernels  223 us (93%)
  other arithmetic  8.66 us (4%)
  local copies, waits for them, and re-layouts  3.77 us (2%)
    pallas_call x1, Pallas kernels, ring_scatter(): pl.pallas_call(functools.partial(scatter_kernel, chips), out_shape=[jax.S...  91.2 us
    pallas_call x1, Pallas kernels, ring_gather(): pl.pallas_call(functools.partial(gather_kernel, chips), out_shape=[jax.Sh...  89.7 us
    pallas_call x1, Pallas kernels, fwd(): pl.pallas_call(functools.partial(fwd_kernel, experts, cap, block, step_pa...  21.6 us
    pallas_call x1, Pallas kernels, bwd(): pl.pallas_call(functools.partial(bwd_kernel, experts, cap, block, step_pa...  20.4 us

profile of v2, /device:TPU:13, one launch (start us, length us, event | category | flops | bytes accessed | tf_op | source)
XLA Modules:
  0.0 235.9 jit_solution(13435248818159792187)
XLA Ops:
  0.6 0.7 broadcast_compare_fusion
  1.3 1.2 fusion.6
  2.5 0.7 convert_element_type.23
  3.2 0.7 fusion.10
  3.9 0.8 fusion.9
  4.7 0.1 copy.16
  4.8 0.1 copy.17
  5.0 0.1 copy.15
  5.1 0.8 copy.14
  5.9 1.3 fusion.7
  7.2 1.0 concatenate.3.a_ref
  8.2 89.7 %shard_map.104 = (bf16[2048,2176]{1,0:T(8,128)(2,1)}, bf16[2048,2048]{1,0:T(8,128)(2,1)}) custom-call(bf16[128,2176]{1,0:T(8,128)(2,1)} %concatenate.3.a_ref, bf16[128,2048]{1,0:T(8,128)(2,1)} %b_ref.1), custom_call_target="tpu_custom_call" | custom-call | tf_op jit(solution)/shard_map/pallas_call | solution.py:209
  97.9 21.6 %shard_map.105 = (bf16[2048,2048]{1,0:T(8,128)(2,1)}, f32[2,640,384]{2,1,0:T(8,128)}, f32[2,640,384]{2,1,0:T(8,128)}, bf16[8,160,256]{2,1,0:T(8,128)(2,1)}, f32[2,640,1]{2,1,0:T(8,128)}) custom-call(bf16[2048,2176]{1,0:T(8,128)(2,1)} %get-tuple-element.11.rows_ref, bf16[2,2048,384]{2,1,0:T(8,128)(2,1)} %wg_ref.3, bf16[2,2048,384]{2,1,0:T(8,128)(2,1)} %wu_ref.3, ...), custom_call_target="tpu_custom_call" | custom-call | flops 12079595520 | bytes 31457280 | tf_op jit(solution)/shard_map/pallas_call | solution.py:348
  119.5 20.4 %shard_map.106.b_ref = bf16[2048,2048]{1,0:T(8,128)(2,1)} custom-call(bf16[2048,2048]{1,0:T(8,128)(2,1)} %get-tuple-element.13.cot_ref, f32[2,640,384]{2,1,0:T(8,128)} %get-tuple-element.14.gate_ref, f32[2,640,384]{2,1,0:T(8,128)} %get-tuple-element.15.up_ref, bf16[8,160,256]{2,1,0:T(8,128)(2,1)} %get-tuple-element.16.tab_ref, ...), custom_call_target="tpu_custom_call" | custom-call | flops 12079595520 | bytes 31457280 | tf_op jit(solution)/shard_map/pallas_call | solution.py:361
  139.8 0.0 copy-start
  139.8 91.2 %shard_map.107 = (bf16[128,2048]{1,0:T(8,128)(2,1)}, f32[128,2048]{1,0:T(8,128)}) custom-call(bf16[2048,2048]{1,0:T(8,128)(2,1)} %get-tuple-element.12.a_ref, bf16[2048,2048]{1,0:T(8,128)(2,1)} %shard_map.106.b_ref), custom_call_target="tpu_custom_call" | custom-call | tf_op jit(solution)/shard_map/pallas_call | solution.py:315
  231.1 0.0 copy-start.1
  231.1 0.0 copy-done
  231.1 1.6 fusion.2
  232.7 2.4 %fusion.5 = bf16[128,2048]{1,0:T(8,128)(2,1)} fusion(bf16[128,2048]{1,0:T(8,128)(2,1)S(1)} %copy-done, f32[128,2048]{1,0:T(8,128)} %get-tuple-element.19, f32[128]{0:T(128)S(1)} %broadcast_multiply_fusion, f32[2048]{0:T(1024)S(1)} %bitcast.7, f32[2048]{0:T(1024)S(1)} %bitcast.4, f32[128]{0:T(128)S(1)} %add_rsqrt_fusion, ...), kind=kLoop, calls=%fused_computation.9 | loop fusion | flops 2097152 | bytes 2114688 | tf_op jit(solution)/shard_map/convert_element_type | solution.py:412
  235.1 0.0 copy-done.1
  235.1 0.8 copy.19
  (4 shorter events, 0.0 us)
Async XLA Ops:
  139.8 91.2 %copy-start = (bf16[128,2048]{1,0:T(8,128)(2,1)S(1)}, bf16[128,2048]{1,0:T(8,128)(2,1)}, u32[]{:S(2)}) copy-start(bf16[128,2048]{1,0:T(8,128)(2,1)} %param.9) | copy-start | bytes 1572868
  231.1 4.1 %copy-start.1 = (bf16[128,2048]{1,0:T(8,128)(2,1)S(1)}, bf16[128,2048]{1,0:T(8,128)(2,1)}, u32[]{:S(2)}) copy-start(bf16[128,2048]{1,0:T(8,128)(2,1)} %get-tuple-element.28) | copy-start | bytes 1572868

commit v3 on v2

--- a/solution.py
+++ b/solution.py
@@ -41,59 +41,81 @@
     return tables, slot_weights
 
 
-def fwd_kernel(experts, cap, block, pairs, top, rows_ref, wg_ref, wu_ref, wd_ref,
-               out_ref, gate_ref, up_ref, tab_ref, sw_ref, picked, weighted):
+def fwd_work(experts, cap, block, all_pairs, pairs, top, rows_ref, wg_ref, wu_ref, wd_ref,
+             out_ref, gate_ref, up_ref, tab_ref, sw_ref, picked, weighted):
     first = lax.axis_index("expert") * experts
     width = wg_ref.shape[1]
     n = 2 * cap
-    for p in range(pairs):
-        meta = rows_ref[p * 2 * block:(p + 1) * 2 * block, width:].astype(F32).T
-        ids = meta[0:top]
-        gates = (meta[top:2 * top] + meta[2 * top:3 * top]) + meta[3 * top:4 * top]
-        tables, slot_weights = pick_table(ids, gates, first.astype(F32), experts, cap, block)
-        full = jnp.concatenate(tables, axis=0).astype(BF16)
-        tab_ref[p] = full
-        got = dot(full, rows_ref[p * 2 * block:(p + 1) * 2 * block, 0:width]).astype(BF16)
+    pair = 2 * block
+    for g in range(0, all_pairs, pairs):
+        for p in range(pairs):
+            at = slice((g + p) * pair, (g + p + 1) * pair)
+            meta = rows_ref[at, width:].astype(F32).T
+            ids = meta[0:top]
+            gates = (meta[top:2 * top] + meta[2 * top:3 * top]) + meta[3 * top:4 * top]
+            tables, slot_weights = pick_table(ids, gates, first.astype(F32), experts, cap, block)
+            full = jnp.concatenate(tables, axis=0).astype(BF16)
+            tab_ref[g + p] = full
+            got = dot(full, rows_ref[at, 0:width]).astype(BF16)
+            for e in range(experts):
+                picked[e, p * n:(p + 1) * n, :] = got[e * n:(e + 1) * n]
+                sw_ref[e, (g + p) * n:(g + p + 1) * n, :] = slot_weights[e]
+        yield
+        span = slice(g * n, (g + pairs) * n)
         for e in range(experts):
-            picked[e, p * n:(p + 1) * n, :] = got[e * n:(e + 1) * n]
-            sw_ref[e, p * n:(p + 1) * n, :] = slot_weights[e]
-    for e in range(experts):
-        gate = dot(picked[e], wg_ref[e])
-        up = dot(picked[e], wu_ref[e])
-        gate_ref[e] = gate
-        up_ref[e] = up
-        hidden = (gate * jax.nn.sigmoid(gate) * up).astype(BF16)
-        res = dot(hidden, wd_ref[e]) * sw_ref[e]
-        res = res.astype(BF16)
+            gate = dot(picked[e], wg_ref[e])
+            up = dot(picked[e], wu_ref[e])
+            gate_ref[e, span, :] = gate
+            up_ref[e, span, :] = up
+            hidden = (gate * jax.nn.sigmoid(gate) * up).astype(BF16)
+            res = (dot(hidden, wd_ref[e]) * sw_ref[e, span, :]).astype(BF16)
+            for p in range(pairs):
+                weighted[p, e * n:(e + 1) * n, :] = res[p * n:(p + 1) * n]
+            yield
         for p in range(pairs):
-            weighted[p, e * n:(e + 1) * n, :] = res[p * n:(p + 1) * n]
-    for p in range(pairs):
-        out_ref[p * 2 * block:(p + 1) * 2 * block, :] = dot(
-            tab_ref[p], weighted[p], ((0,), (0,))).astype(BF16)
-
-
-def bwd_kernel(experts, cap, block, pairs, cot_ref, gate_ref, up_ref, tab_ref, sw_ref,
-               wg_ref, wu_ref, wd_ref, out_ref, picked, weighted):
+            out_ref[(g + p) * pair:(g + p + 1) * pair, :] = dot(
+                tab_ref[g + p], weighted[p], ((0,), (0,))).astype(BF16)
+        yield
+
+
+def bwd_work(experts, cap, block, all_pairs, pairs, cot_ref, gate_ref, up_ref, tab_ref, sw_ref,
+             wg_ref, wu_ref, wd_ref, out_ref, picked, weighted):
     n = 2 * cap
+    pair = 2 * block
     tr = ((1,), (1,))
-    for p in range(pairs):
-        got = dot(tab_ref[p], cot_ref[p * 2 * block:(p + 1) * 2 * block, :])
+    for g in range(0, all_pairs, pairs):
+        for p in range(pairs):
+            got = dot(tab_ref[g + p], cot_ref[(g + p) * pair:(g + p + 1) * pair, :])
+            for e in range(experts):
+                picked[e, p * n:(p + 1) * n, :] = (
+                    got[e * n:(e + 1) * n] * sw_ref[e, (g + p) * n:(g + p + 1) * n, :]).astype(BF16)
+        yield
+        span = slice(g * n, (g + pairs) * n)
         for e in range(experts):
-            picked[e, p * n:(p + 1) * n, :] = (
-                got[e * n:(e + 1) * n] * sw_ref[e, p * n:(p + 1) * n, :]).astype(BF16)
-    for e in range(experts):
-        hidden_grad = dot(picked[e], wd_ref[e], tr)
-        gate = gate_ref[e]
-        up = up_ref[e]
-        sig = jax.nn.sigmoid(gate)
-        pre_grad = (hidden_grad * up * sig * (1.0 + gate * (1.0 - sig))).astype(BF16)
-        up_grad = (hidden_grad * gate * sig).astype(BF16)
-        res = (dot(pre_grad, wg_ref[e], tr) + dot(up_grad, wu_ref[e], tr)).astype(BF16)
+            hidden_grad = dot(picked[e], wd_ref[e], tr)
+            gate = gate_ref[e, span, :]
+            up = up_ref[e, span, :]
+            sig = jax.nn.sigmoid(gate)
+            pre_grad = (hidden_grad * up * sig * (1.0 + gate * (1.0 - sig))).astype(BF16)
+            up_grad = (hidden_grad * gate * sig).astype(BF16)
+            res = (dot(pre_grad, wg_ref[e], tr) + dot(up_grad, wu_ref[e], tr)).astype(BF16)
+            for p in range(pairs):
+                weighted[p, e * n:(e + 1) * n, :] = res[p * n:(p + 1) * n]
+            yield
         for p in range(pairs):
-            weighted[p, e * n:(e + 1) * n, :] = res[p * n:(p + 1) * n]
-    for p in range(pairs):
-        out_ref[p * 2 * block:(p + 1) * 2 * block, :] = dot(
-            tab_ref[p], weighted[p], ((0,), (0,))).astype(BF16)
+            out_ref[(g + p) * pair:(g + p + 1) * pair, :] = dot(
+                tab_ref[g + p], weighted[p], ((0,), (0,))).astype(BF16)
+        yield
+
+
+def fwd_kernel(experts, cap, block, pairs, top, *refs):
+    for unused in fwd_work(experts, cap, block, pairs, pairs, top, *refs):
+        pass
+
+
+def bwd_kernel(experts, cap, block, pairs, *refs):
+    for unused in bwd_work(experts, cap, block, pairs, pairs, *refs):
+        pass
 
 
 def ring_place(chips):
@@ -138,16 +160,15 @@
         device_id={"expert": peer}, device_id_type=pl.DeviceIdType.MESH)
 
 
-def gather_kernel(chips, a_ref, b_ref, oa_ref, ob_ref, ring_s, ring_r, pair_s, pair_r, own_s):
+def gather_body(chips, ins, outs, ring_s, ring_r, pair_s, pair_r, own_s, work=()):
+    work = iter(work)
     place, core, index = ring_place(chips)
     steps = (1, -1)
     peers = [index(place + 1, core), index(place - 1, core)]
     partner = index(place, 1 - core)
     enter(peers + [partner])
-    block = a_ref.shape[0]
+    block = ins[0].shape[0]
     half = block // 2
-    ins = (a_ref, b_ref)
-    outs = (oa_ref, ob_ref)
     order = pieces(chips)
     count = len(order[0])
 
@@ -158,7 +179,7 @@
     waits = []
     own = []
     for j in range(2):
-        for x in range(2):
+        for x in range(len(ins)):
             for way in range(2):
                 d, h = order[way][j]
                 here = rows(core, place, h)
@@ -166,7 +187,7 @@
                                ring_s.at[x, way, j], ring_r.at[x, way, j], peers[way])
                 copy.start()
                 waits.append(copy)
-    for x in range(2):
+    for x in range(len(ins)):
         here = pl.ds(pl.multiple_of(index(place, core) * block, block), block)
         copy = pltpu.make_async_copy(ins[x], outs[x].at[here, :], own_s.at[x])
         copy.start()
@@ -174,8 +195,9 @@
         copy = send_to(ins[x], outs[x].at[here, :], pair_s.at[x, 2, 0], pair_r.at[x, 2, 0], partner)
         copy.start()
         waits.append(copy)
+    next(work, None)
     for j in range(count):
-        for x in range(2):
+        for x in range(len(ins)):
             for way in range(2):
                 d, h = order[way][j]
                 got = outs[x].at[rows(core, place - steps[way] * d, h), :]
@@ -188,11 +210,14 @@
                 copy = send_to(got, got, pair_s.at[x, way, j], pair_r.at[x, way, j], partner)
                 copy.start()
                 waits.append(copy)
+        next(work, None)
+    for unused in work:
+        pass
     for copy in waits:
         copy.wait_send()
     for copy in own:
         copy.wait()
-    for x in range(2):
+    for x in range(len(ins)):
         here = outs[x].at[pl.ds(pl.multiple_of(index(place, 1 - core) * block, block), block), :]
         send_to(here, here, pair_s.at[x, 2, 0], pair_r.at[x, 2, 0], partner).wait_recv()
         for j in range(count):
@@ -202,32 +227,80 @@
                 send_to(here, here, pair_s.at[x, way, j], pair_r.at[x, way, j], partner).wait_recv()
 
 
-def ring_gather(a, b, devices):
+def gather_sems(arrays, count):
+    sems = pltpu.SemaphoreType.DMA
+    return [sems((arrays, 2, count)), sems((arrays, 2, count)), sems((arrays, 3, count)),
+            sems((arrays, 3, count)), sems((arrays,))]
+
+
+def gather_kernel(chips, a_ref, oa_ref, *scratch):
+    gather_body(chips, (a_ref,), (oa_ref,), *scratch)
+
+
+VM = pl.BlockSpec(memory_space=pltpu.VMEM)
+ANY = pl.BlockSpec(memory_space=pl.ANY)
+
+
+def ring_gather(a, devices):
     chips = devices // 2
-    count = chips - 1
-    sems = pltpu.SemaphoreType.DMA
     return pl.pallas_call(
         functools.partial(gather_kernel, chips),
-        out_shape=[jax.ShapeDtypeStruct((devices * x.shape[0], x.shape[1]), x.dtype) for x in (a, b)],
-        in_specs=[pl.BlockSpec(memory_space=pltpu.VMEM)] * 2,
-        out_specs=[pl.BlockSpec(memory_space=pl.ANY)] * 2,
-        scratch_shapes=[sems((2, 2, count)), sems((2, 2, count)), sems((2, 3, count)),
-                        sems((2, 3, count)), sems((2,))],
+        out_shape=jax.ShapeDtypeStruct((devices * a.shape[0], a.shape[1]), a.dtype),
+        in_specs=[VM], out_specs=ANY,
+        scratch_shapes=gather_sems(1, chips - 1),
         compiler_params=pltpu.CompilerParams(collective_id=0, has_side_effects=True),
-    )(a, b)
-
-
-def scatter_kernel(chips, a_ref, b_ref, oa_ref, ob_ref, pair_buf, send_buf, recv_buf,
-                   ring_s, ring_r, pair_s, pair_r):
+    )(a)
+
+
+def fwd_gather_kernel(chips, experts, cap, block, pairs, top, cot_ref, rows_ref, wg_ref, wu_ref, wd_ref,
+                      cots_ref, out_ref, gate_ref, up_ref, tab_ref, sw_ref, rows, wg, wu, wd,
+                      picked, weighted, load_s, *sems):
+    loads = [pltpu.make_async_copy(src, dst, load_s.at[i]) for i, (src, dst) in enumerate(
+        ((rows_ref, rows), (wg_ref, wg), (wu_ref, wu), (wd_ref, wd)))]
+    for load in loads:
+        load.start()
+
+    def work():
+        for load in loads:
+            load.wait()
+        yield from fwd_work(experts, cap, block, chips, pairs, top, rows, wg, wu, wd,
+                            out_ref, gate_ref, up_ref, tab_ref, sw_ref, picked, weighted)
+
+    gather_body(chips, (cot_ref,), (cots_ref,), *sems, work=work())
+
+
+def fwd_gather(cot, rows, weights, cap, top, devices, pairs):
+    chips = devices // 2
+    experts, width, ff = weights[0].shape
+    block = cot.shape[0]
+    n = 2 * cap
+    pre = jax.ShapeDtypeStruct((experts, chips * n, ff), F32)
+    return pl.pallas_call(
+        functools.partial(fwd_gather_kernel, chips, experts, cap, block, pairs, top),
+        out_shape=[jax.ShapeDtypeStruct((devices * block, width), BF16),
+                   jax.ShapeDtypeStruct((devices * block, width), BF16), pre, pre,
+                   jax.ShapeDtypeStruct((chips, experts * n, 2 * block), BF16),
+                   jax.ShapeDtypeStruct((experts, chips * n, 1), F32)],
+        in_specs=[VM, ANY, ANY, ANY, ANY],
+        out_specs=[ANY, VM, VM, VM, VM, VM],
+        scratch_shapes=[pltpu.VMEM(rows.shape, BF16)] + [pltpu.VMEM(w.shape, BF16) for w in weights] + [
+            pltpu.VMEM((experts, pairs * n, width), BF16), pltpu.VMEM((pairs, experts * n, width), BF16),
+            pltpu.SemaphoreType.DMA((4,))] + gather_sems(1, chips - 1),
+        compiler_params=pltpu.CompilerParams(collective_id=2, has_side_effects=True,
+                                             vmem_limit_bytes=60 << 20),
+    )(cot, rows, *weights)
+
+
+def scatter_body(chips, ins, outs, pair_buf, send_buf, recv_buf, ring_s, ring_r, pair_s, pair_r,
+                 work=()):
+    work = iter(work)
     place, core, index = ring_place(chips)
     steps = (1, -1)
     peers = [index(place + 1, core), index(place - 1, core)]
     partner = index(place, 1 - core)
     enter(peers + [partner])
-    block = oa_ref.shape[0]
+    block = outs[0].shape[0]
     half = block // 2
-    ins = (a_ref, b_ref)
-    outs = (oa_ref, ob_ref)
     far = chips // 2
     order = [row[::-1] for row in pieces(chips)]
     count = len(order[0])
@@ -239,7 +312,7 @@
     slot_of[-far] = 0
     pair_copies = {}
     for i, o in enumerate(offsets):
-        for x in range(2):
+        for x in range(len(ins)):
             theirs = pl.ds(pl.multiple_of(index(place + o, 1 - core) * block, block), block)
             copy = send_to(ins[x].at[theirs, :], pair_buf.at[x, i], pair_s.at[x, i],
                            pair_r.at[x, i], partner)
@@ -272,7 +345,7 @@
 
     sends = {}
     for j in range(count):
-        for x in range(2):
+        for x in range(len(ins)):
             for way in range(2):
                 d, h = order[way][j]
                 more = []
@@ -289,7 +362,10 @@
                                ring_s.at[x, way, j], ring_r.at[x, way, j], peers[way])
                 copy.start()
                 sends[x, way, j] = copy
-    for x in range(2):
+        next(work, None)
+    for unused in work:
+        pass
+    for x in range(len(ins)):
         for h in range(2):
             more = []
             for way in range(2):
@@ -307,23 +383,66 @@
         copy.wait_send()
 
 
-def ring_scatter(a, b, devices):
+def scatter_scratch(arrays, chips, block, width):
+    count = chips - 1
+    sems = pltpu.SemaphoreType.DMA
+    return [pltpu.VMEM((arrays, chips, block, width), BF16),
+            pltpu.VMEM((arrays, 2, count, block // 2, width), BF16),
+            pltpu.VMEM((arrays, 2, count, block // 2, width), BF16),
+            sems((arrays, 2, count)), sems((arrays, 2, count)), sems((arrays, chips)),
+            sems((arrays, chips))]
+
+
+def scatter_kernel(chips, a_ref, oa_ref, *scratch):
+    scatter_body(chips, (a_ref,), (oa_ref,), *scratch)
+
+
+def ring_scatter(a, devices):
     chips = devices // 2
-    count = chips - 1
     block, width = a.shape[0] // devices, a.shape[1]
-    sems = pltpu.SemaphoreType.DMA
     return pl.pallas_call(
         functools.partial(scatter_kernel, chips),
-        out_shape=[jax.ShapeDtypeStruct((block, width), BF16), jax.ShapeDtypeStruct((block, width), F32)],
-        in_specs=[pl.BlockSpec(memory_space=pltpu.VMEM)] * 2,
-        out_specs=[pl.BlockSpec(memory_space=pltpu.VMEM)] * 2,
-        scratch_shapes=[pltpu.VMEM((2, chips, block, width), BF16),
-                        pltpu.VMEM((2, 2, count, block // 2, width), BF16),
-                        pltpu.VMEM((2, 2, count, block // 2, width), BF16),
-                        sems((2, 2, count)), sems((2, 2, count)), sems((2, chips)), sems((2, chips))],
+        out_shape=jax.ShapeDtypeStruct((block, width), F32),
+        in_specs=[VM], out_specs=VM,
+        scratch_shapes=scatter_scratch(1, chips, block, width),
         compiler_params=pltpu.CompilerParams(collective_id=1, has_side_effects=True,
-                                             vmem_limit_bytes=62 << 20),
-    )(a, b)
+                                             vmem_limit_bytes=40 << 20),
+    )(a)
+
+
+def bwd_scatter_kernel(chips, experts, cap, block, pairs, part_ref, cots_ref, gate_ref, up_ref, tab_ref,
+                       sw_ref, wg_ref, wu_ref, wd_ref, moe_ref, out_ref, cots, wg, wu, wd,
+                       picked, weighted, load_s, *scratch):
+    loads = [pltpu.make_async_copy(src, dst, load_s.at[i]) for i, (src, dst) in enumerate(
+        ((cots_ref, cots), (wg_ref, wg), (wu_ref, wu), (wd_ref, wd)))]
+    for load in loads:
+        load.start()
+
+    def work():
+        for load in loads:
+            load.wait()
+        yield from bwd_work(experts, cap, block, chips, pairs, cots, gate_ref, up_ref, tab_ref, sw_ref,
+                            wg, wu, wd, out_ref, picked, weighted)
+
+    scatter_body(chips, (part_ref,), (moe_ref,), *scratch, work=work())
+
+
+def bwd_scatter(part, cots, gate_pre, up_pre, table, slot_weights, weights, cap, devices, pairs):
+    chips = devices // 2
+    experts, width, ff = weights[0].shape
+    block = part.shape[0] // devices
+    n = 2 * cap
+    return pl.pallas_call(
+        functools.partial(bwd_scatter_kernel, chips, experts, cap, block, pairs),
+        out_shape=[jax.ShapeDtypeStruct((block, width), BF16), jax.ShapeDtypeStruct(part.shape, BF16)],
+        in_specs=[VM, ANY, VM, VM, VM, VM, ANY, ANY, ANY],
+        out_specs=[VM, VM],
+        scratch_shapes=[pltpu.VMEM(cots.shape, BF16)] + [pltpu.VMEM(w.shape, BF16) for w in weights] + [
+            pltpu.VMEM((experts, pairs * n, width), BF16), pltpu.VMEM((pairs, experts * n, width), BF16),
+            pltpu.SemaphoreType.DMA((4,))] + scatter_scratch(1, chips, block, width),
+        compiler_params=pltpu.CompilerParams(collective_id=3, has_side_effects=True,
+                                             vmem_limit_bytes=67043328),
+    )(part, cots, gate_pre, up_pre, table, slot_weights, *weights)
 
 
 def expert_calls(devices, top, weights, block, cap, step_pairs):
@@ -392,18 +511,19 @@
         [normed, expert_ids.astype(BF16), high.astype(BF16), middle.astype(BF16), low.astype(BF16), pad],
         axis=1)
     by_ring = devices % 4 == 0 and devices * block * width * 2 * 2 <= 20 << 20
+    weights = (w_gate, w_up, w_down)
     if by_ring:
-        rows, cots = ring_gather(normed, cotangent, devices)
+        rows = ring_gather(normed, devices)
+        cots, out_part, *saved = fwd_gather(cotangent, rows, weights, cap, top, devices, 4)
+        moe_out, grad_part = bwd_scatter(out_part, cots, *saved, weights, cap, devices, 2)
+        normed_grad = ring_scatter(grad_part, devices)
     else:
         rows = lax.all_gather(normed, "expert", axis=0, tiled=True)
         cots = lax.all_gather(cotangent, "expert", axis=0, tiled=True)
-    fwd, bwd = expert_calls(devices, top, (w_gate, w_up, w_down), block, cap, 4)
-    out_part, gate_pre, up_pre, table, slot_weights = fwd(rows)
-    grad_part = bwd(cots, gate_pre, up_pre, table, slot_weights)
-    if by_ring:
-        moe_out, normed_grad = ring_scatter(out_part, grad_part, devices)
-    else:
+        fwd, bwd = expert_calls(devices, top, weights, block, cap, 4)
+        out_part, *saved = fwd(rows)
         moe_out = lax.psum_scatter(out_part, "expert", scatter_dimension=0, tiled=True)
+        grad_part = bwd(cots, *saved)
         normed_grad = lax.psum_scatter(grad_part, "expert", scatter_dimension=0, tiled=True)
     scaled = normed_grad.astype(F32) * gain_rows
     grad_input = inv_rms * (

time: 239 us -> 215 us (0.90)
  Pallas kernels: 223 us -> 198 us
  local copies, waits for them, and re-layouts: 3.77 us -> 7.18 us
  other arithmetic: 8.66 us -> 6.15 us
    pallas_call x4, Pallas kernels: 223 us -> 198 us  [the longest x1 52.7 us: bwd_scatter(): pl.pallas_call(functools.partial(bwd_scatter_kernel, chips, experts, cap,...]
    unnamed x6 -> x24, local copies, waits for them, and re-layouts: 1.59 us -> 5 us
where the time goes in v3:
time: 215 us; the launch traced here: 212 us
  Pallas kernels  198 us (92%)
  local copies, waits for them, and re-layouts  7.18 us (3%)
  other arithmetic  6.15 us (3%)
    pallas_call x1, Pallas kernels, bwd_scatter(): pl.pallas_call(functools.partial(bwd_scatter_kernel, chips, experts, cap,...  52.7 us
    pallas_call x1, Pallas kernels, fwd_gather(): pl.pallas_call(functools.partial(fwd_gather_kernel, chips, experts, cap,...  50.9 us
    pallas_call x1, Pallas kernels, ring_gather(): pl.pallas_call(functools.partial(gather_kernel, chips), out_shape=jax.Sha...  49.6 us
    pallas_call x1, Pallas kernels, ring_scatter(): pl.pallas_call(functools.partial(scatter_kernel, chips), out_shape=jax.Sh...  44.8 us
    unnamed x24, local copies, waits for them, and re-layouts  5 us

profile of v3, /device:TPU:13, one launch (start us, length us, event | category | flops | bytes accessed | tf_op | source)
XLA Modules:
  0.0 212.1 jit_solution(9442922763233926436)
XLA Ops:
  0.6 0.7 broadcast_compare_fusion
  1.3 0.0 copy-start.7
  1.3 1.2 fusion.6
  2.5 0.0 copy-start.9
  2.5 0.7 convert_element_type.23
  3.2 0.7 fusion.10
  3.9 0.8 fusion.9
  4.7 0.0 copy-start.3
  4.7 0.0 copy-start.5
  4.8 0.1 copy.16
  4.9 0.1 copy.17
  5.0 0.1 copy.15
  5.1 0.8 copy.14
  5.9 0.0 copy-done.7
  5.9 0.0 copy-done.9
  5.9 1.3 fusion.7
  7.3 1.0 concatenate.3.a_ref
  8.3 49.6 %shard_map.104.rows_ref = bf16[2048,2176]{1,0:T(8,128)(2,1)} custom-call(bf16[128,2176]{1,0:T(8,128)(2,1)} %concatenate.3.a_ref), custom_call_target="tpu_custom_call" | custom-call | tf_op jit(solution)/shard_map/pallas_call | solution.py:246
  57.9 0.0 copy-done.3
  57.9 0.0 copy-done.5
  57.9 50.9 %shard_map.105 = (bf16[2048,2048]{1,0:T(8,128)(2,1)}, bf16[2048,2048]{1,0:T(8,128)(2,1)}, f32[2,640,384]{2,1,0:T(8,128)}, f32[2,640,384]{2,1,0:T(8,128)}, bf16[8...) custom-call(bf16[128,2048]{1,0:T(8,128)(2,1)} %cot_ref.1, bf16[2048,2176]{1,0:T(8,128)(2,1)} %shard_map.104.rows_ref, ...), custom_call_target="tpu_custom_call" | custom-call | tf_op jit(solution)/shard_map/pallas_call | solution.py:278
  108.8 52.7 %shard_map.106 = (bf16[128,2048]{1,0:T(8,128)(2,1)}, bf16[2048,2048]{1,0:T(8,128)(2,1)}) custom-call(bf16[2048,2048]{1,0:T(8,128)(2,1)} %get-tuple-element.10.part_ref, bf16[2048,2048]{1,0:T(8,128)(2,1)} %get-tuple-element.11.cots_ref, f32[2,640,384]{2,1,0:T(8,128)} %get-tuple-element.12.gate_ref, f32[2,640,384]{2,1,0:T(8,128)} %get-tuple-element.13.up_ref, ...), custom_call_target="tpu_custom_call" | custom-call | tf_op jit(solution)/shard_map/pallas_call | solution.py:435
  161.5 0.0 copy-start
  161.5 3.4 %copy-done = bf16[2048,2048]{1,0:T(8,128)(2,1)S(1)} copy-done((bf16[2048,2048]{1,0:T(8,128)(2,1)S(1)}, bf16[2048,2048]{1,0:T(8,128)(2,1)}, u32[]{:S(2)}) %copy-start) | copy-done | bytes 8388632
  164.8 0.0 copy-start.1
  164.8 0.0 copy-start.4
  164.8 0.0 copy-start.6
  164.9 0.0 copy-start.8
  164.9 0.0 copy-start.10
  164.9 44.8 %shard_map.107 = f32[128,2048]{1,0:T(8,128)S(1)} custom-call(bf16[2048,2048]{1,0:T(8,128)(2,1)S(1)} %copy-done), custom_call_target="tpu_custom_call" | custom-call | tf_op jit(solution)/shard_map/pallas_call | solution.py:403
  209.7 0.0 copy-done.1
  209.7 0.0 copy-done.4
  209.7 0.0 copy-done.6
  209.8 0.0 copy-done.8
  209.8 0.0 copy-done.10
  209.8 0.0 copy-start.2
  209.8 0.4 fusion.2
  210.2 1.2 fusion.5
  211.3 0.0 copy-done.2
  211.3 0.8 copy.19
  (4 shorter events, 0.0 us)
Async XLA Ops:
  1.3 4.6 %copy-start.7 = (pred[128]{0:T(512)(128)(4,1)}, pred[128]{0:T(512)(128)(4,1)S(1)}, u32[]{:S(2)}) copy-start(pred[128]{0:T(512)(128)(4,1)S(1)} %broadcast_compare_fusion) | copy-start | bytes 388
  2.5 3.4 %copy-start.9 = (f32[128]{0:T(128)}, f32[128]{0:T(128)S(1)}, u32[]{:S(2)}) copy-start(f32[128]{0:T(128)S(1)} %add_rsqrt_fusion) | copy-start | bytes 1540
  4.7 53.1 %copy-start.3 = (f32[1,2048]{1,0:T(1,128)}, f32[1,2048]{1,0:T(1,128)S(1)}, u32[]{:S(2)}) copy-start(f32[1,2048]{1,0:T(1,128)S(1)} %get-tuple-element.20) | copy-start | bytes 24580
  4.7 53.1 %copy-start.5 = (f32[1,2048]{1,0:T(1,128)}, f32[1,2048]{1,0:T(1,128)S(1)}, u32[]{:S(2)}) copy-start(f32[1,2048]{1,0:T(1,128)S(1)} %get-tuple-element.21) | copy-start | bytes 24580
  161.5 3.4 %copy-start = (bf16[2048,2048]{1,0:T(8,128)(2,1)S(1)}, bf16[2048,2048]{1,0:T(8,128)(2,1)}, u32[]{:S(2)}) copy-start(bf16[2048,2048]{1,0:T(8,128)(2,1)} %get-tuple-element.17.a_ref) | copy-start | bytes 25165828
  164.8 44.9 %copy-start.1 = (bf16[128,2048]{1,0:T(8,128)(2,1)S(1)}, bf16[128,2048]{1,0:T(8,128)(2,1)}, u32[]{:S(2)}) copy-start(bf16[128,2048]{1,0:T(8,128)(2,1)} %param.9) | copy-start | bytes 1572868
  164.8 44.9 %copy-start.4 = (f32[1,2048]{1,0:T(1,128)S(1)}, f32[1,2048]{1,0:T(1,128)}, u32[]{:S(2)}) copy-start(f32[1,2048]{1,0:T(1,128)} %copy-done.3) | copy-start | bytes 24580
  164.8 44.9 %copy-start.6 = (f32[1,2048]{1,0:T(1,128)S(1)}, f32[1,2048]{1,0:T(1,128)}, u32[]{:S(2)}) copy-start(f32[1,2048]{1,0:T(1,128)} %copy-done.5) | copy-start | bytes 24580
  164.9 44.9 %copy-start.8 = (pred[128]{0:T(512)(128)(4,1)S(1)}, pred[128]{0:T(512)(128)(4,1)}, u32[]{:S(2)}) copy-start(pred[128]{0:T(512)(128)(4,1)} %copy-done.7) | copy-start | bytes 388
  164.9 44.9 %copy-start.10 = (f32[128]{0:T(128)S(1)}, f32[128]{0:T(128)}, u32[]{:S(2)}) copy-start(f32[128]{0:T(128)} %copy-done.9) | copy-start | bytes 1540
  209.8 1.6 copy-start.2
